TPU v7x, 32 devices: a whole 2x2x4 slice. The times are simulated.
32 devices in a mesh: fsdp: 8 (over y, x, core), ctx: 4 (over z).
Axes of the slice: x: 2, y: 2, z: 4, core: 2. Of those that a mesh axis runs over, the one named last changes fastest.
Arguments:
- inputs: bfloat16 [8, 4096, 1024], P('fsdp', 'ctx'), may hold values from -6 to 6
- cotangent: bfloat16 [8, 4096, 1024], P('fsdp', 'ctx'), may hold values from -6 to 6
- positions: int32 [8, 4096], P('fsdp', 'ctx'), may hold values from 0 to 2303, as said below
- segments: int32 [8, 4096], P('fsdp', 'ctx'), may hold values from 0 to 8, as said below
- ln1_gain: bfloat16 [1024], P('fsdp'), may hold values from 0.5 to 1.5
- ln1_bias: bfloat16 [1024], P('fsdp'), may hold values from -2.5 to 2.5
- w_qkv: bfloat16 [1024, 3072], P('fsdp'), may hold values from -0.1875 to 0.1875
- b_qkv: bfloat16 [3072], P('fsdp'), may hold values from -3 to 3
- w_attn_out: bfloat16 [1024, 1024], P('fsdp'), may hold values from -1.5 to 1.5
- b_out: bfloat16 [1024], P('fsdp'), may hold values from -2.5 to 2.5
- ln2_gain: bfloat16 [1024], P('fsdp'), may hold values from 0.5 to 1.5
- ln2_bias: bfloat16 [1024], P('fsdp'), may hold values from -2.5 to 2.5
- w_in: bfloat16 [1024, 4096], P('fsdp'), may hold values from -0.1875 to 0.1875
- b_in: bfloat16 [4096], P('fsdp'), may hold values from -2.5 to 2.5
- w_out: bfloat16 [4096, 1024], P('fsdp'), may hold values from -0.09375 to 0.09375
Outputs:
- output: bfloat16 [8, 4096, 1024], P('fsdp', 'ctx')
- grad_inputs: float32 [8, 4096, 1024], P('fsdp', 'ctx')
- grad_ln1_gain: float32 [1024], P(('fsdp', 'ctx'))
- grad_ln1_bias: float32 [1024], P(('fsdp', 'ctx'))
- grad_w_qkv: float32 [1024, 3072], P(('fsdp', 'ctx'))
- grad_b_qkv: float32 [3072], P(('fsdp', 'ctx'))
- grad_w_attn_out: float32 [1024, 1024], P(('fsdp', 'ctx'))
- grad_b_out: float32 [1024], P(('fsdp', 'ctx'))
- grad_ln2_gain: float32 [1024], P(('fsdp', 'ctx'))
- grad_ln2_bias: float32 [1024], P(('fsdp', 'ctx'))
- grad_w_in: float32 [1024, 4096], P(('fsdp', 'ctx'))
- grad_b_in: float32 [4096], P(('fsdp', 'ctx'))
- grad_w_out: float32 [4096, 1024], P(('fsdp', 'ctx'))
Inputs may be any that keep to these rules, and one draw needn't show every extreme that they name: `positions`: in a group, token t of the natural order (the prompt, then the continuations one after another) has position t and segment 0 if t < 2048, else position 2048 + (t - 2048) % 256 and segment 1 + (t - 2048) // 256. The natural order is cut into 8 blocks of 512 tokens; index j of ctx holds block p_j followed by block 7 - p_j, where p is a permutation of 0 to 3 drawn for each group. `segments`: laid out with positions as stated there.
All inputs are finite; a program needn't handle non-finite values.
Results may differ from a plain program's by a relative error of at most 0.014.
Values may be sent and summed in bfloat16 or wider, within the bound.
No kernel may reach another device: no remote copies, remote signals or barrier semaphores. Data moves between devices by JAX's collectives and lax.ppermute only.
A program may use at most 256 MiB of HBM per device.

v0:
```python
from functools import partial
import math
import jax
import jax.numpy as jnp
from jax import lax
from jax.sharding import PartitionSpec as P

HEADS = 16
HD = 64
ROT = 16
NORM_EPS = 1e-05
MASKED = -1e30


def layer_norm(values, scaling, offset):
    average = jnp.mean(values, axis=-1, keepdims=True)
    centered = values - average
    variance = jnp.mean(centered * centered, axis=-1, keepdims=True)
    return centered * lax.rsqrt(variance + NORM_EPS) * scaling + offset


def rotary_tables(positions):
    halfway = ROT // 2
    spacing = jnp.arange(halfway, dtype=jnp.float32) * (2.0 / ROT)
    inverse = jnp.exp(-math.log(10000.0) * spacing)
    angles = positions.astype(jnp.float32)[..., None] * inverse
    return (jnp.cos(angles), jnp.sin(angles))


def rotate(heads_in, cosine, sine):
    halfway = ROT // 2
    cosine = cosine[..., None, :]
    sine = sine[..., None, :]
    first = heads_in[..., :halfway]
    second = heads_in[..., halfway:ROT]
    return jnp.concatenate(
        [first * cosine - second * sine, second * cosine + first * sine, heads_in[..., ROT:]],
        axis=-1,
    )


def unrotate(grads_in, cosine, sine):
    halfway = ROT // 2
    cosine = cosine[..., None, :]
    sine = sine[..., None, :]
    first = grads_in[..., :halfway]
    second = grads_in[..., halfway:ROT]
    return jnp.concatenate(
        [first * cosine + second * sine, second * cosine - first * sine, grads_in[..., ROT:]],
        axis=-1,
    )


def allowed_mask(query_pos, query_seg, key_pos, key_seg):
    same_doc = (key_seg[:, None, :] == 0) | (key_seg[:, None, :] == query_seg[:, :, None])
    causal = key_pos[:, None, :] <= query_pos[:, :, None]
    return (same_doc & causal)[:, None]


def scores_of(queries, keys_blk):
    return jnp.einsum("gqhd,gkhd->ghqk", queries, keys_blk, preferred_element_type=jnp.float32)


def block_grads(queries, grad_att, log_total, delta, mask, keys_blk, values_blk):
    probs = jnp.where(mask, jnp.exp(scores_of(queries, keys_blk) - log_total[..., None]), 0.0)
    dprobs = jnp.einsum("gqhd,gkhd->ghqk", grad_att, values_blk, preferred_element_type=jnp.float32)
    grad_scores = (probs * (dprobs - delta[..., None])).astype(jnp.bfloat16)
    return (probs.astype(jnp.bfloat16), grad_scores)


def local(
    inputs,
    cotangent,
    positions,
    segments,
    ln1_gain,
    ln1_bias,
    w_qkv,
    b_qkv,
    w_attn_out,
    b_out,
    ln2_gain,
    ln2_bias,
    w_in,
    b_in,
    w_out,
):
    shards = (
        ln1_gain,
        ln1_bias,
        w_qkv,
        b_qkv,
        w_attn_out,
        b_out,
        ln2_gain,
        ln2_bias,
        w_in,
        b_in,
        w_out,
    )
    params = (
        lax.all_gather(shards[0], "fsdp", axis=0, tiled=True),
        lax.all_gather(shards[1], "fsdp", axis=0, tiled=True),
        lax.all_gather(shards[2], "fsdp", axis=0, tiled=True),
        lax.all_gather(shards[3], "fsdp", axis=0, tiled=True),
        lax.all_gather(shards[4], "fsdp", axis=0, tiled=True),
        lax.all_gather(shards[5], "fsdp", axis=0, tiled=True),
        lax.all_gather(shards[6], "fsdp", axis=0, tiled=True),
        lax.all_gather(shards[7], "fsdp", axis=0, tiled=True),
        lax.all_gather(shards[8], "fsdp", axis=0, tiled=True),
        lax.all_gather(shards[9], "fsdp", axis=0, tiled=True),
        lax.all_gather(shards[10], "fsdp", axis=0, tiled=True),
    )
    groups, local_len, width = inputs.shape
    rows_total = groups * local_len
    block = math.gcd(local_len, 256)
    label_pos, label_seg = (
        lax.all_gather(positions, "ctx", axis=1, tiled=True),
        lax.all_gather(segments, "ctx", axis=1, tiled=True),
    )
    count = label_pos.shape[1] // block
    f32 = jnp.float32
    bf16 = jnp.bfloat16
    (
        gain_attn,
        shift_attn,
        weight_qkv,
        bias_qkv,
        weight_attn,
        bias_out,
        gain_mlp,
        shift_mlp,
        weight_in,
        bias_in,
        weight_out,
    ) = params
    flat_in = inputs.reshape(rows_total, width).astype(f32)
    normed_attn = layer_norm(flat_in, gain_attn.astype(f32), shift_attn.astype(f32)).astype(bf16)
    normed_mlp = layer_norm(flat_in, gain_mlp.astype(f32), shift_mlp.astype(f32)).astype(bf16)
    projected = jnp.dot(normed_attn, weight_qkv, preferred_element_type=f32) + bias_qkv.astype(f32)
    cosine, sine = rotary_tables(positions)

    def split_heads(columns):
        return columns.reshape(groups, local_len, HEADS, HD)

    scale = HD ** (-0.5)
    queries = (rotate(split_heads(projected[:, :width]), cosine, sine) * scale).astype(bf16)
    keys_own = rotate(split_heads(projected[:, width : 2 * width]), cosine, sine).astype(bf16)
    values_own = split_heads(projected[:, 2 * width :]).astype(bf16)
    keys_all, values_all = (
        lax.all_gather(keys_own, "ctx", axis=1, tiled=True),
        lax.all_gather(values_own, "ctx", axis=1, tiled=True),
    )

    def key_block(index):
        start = index * block
        keys_blk = lax.dynamic_slice_in_dim(keys_all, start, block, 1)
        values_blk = lax.dynamic_slice_in_dim(values_all, start, block, 1)
        mask = allowed_mask(
            positions,
            segments,
            lax.dynamic_slice_in_dim(label_pos, start, block, 1),
            lax.dynamic_slice_in_dim(label_seg, start, block, 1),
        )
        return (keys_blk, values_blk, mask)

    def total_step(carry, index):
        peak, total = carry
        keys_blk, values_blk, mask = key_block(index)
        scores = jnp.where(mask, scores_of(queries, keys_blk), MASKED)
        fresh = jnp.maximum(peak, jnp.max(scores, axis=-1))
        added = jnp.sum(jnp.where(mask, jnp.exp(scores - fresh[..., None]), 0.0), axis=-1)
        return ((fresh, total * jnp.exp(peak - fresh) + added), None)

    stat_shape = (groups, HEADS, local_len)
    (peak, total), unused = lax.scan(
        total_step,
        (jnp.full(stat_shape, MASKED, f32), jnp.zeros(stat_shape, f32)),
        jnp.arange(count),
    )
    log_total = peak + jnp.log(total)

    def attend_step(rounded_sum, index):
        keys_blk, values_blk, mask = key_block(index)
        probs = jnp.where(mask, jnp.exp(scores_of(queries, keys_blk) - log_total[..., None]), 0.0)
        rounded_sum = rounded_sum + jnp.einsum(
            "ghqk,gkhd->gqhd", probs.astype(bf16), values_blk, preferred_element_type=f32
        )
        return (rounded_sum, None)

    head_shape = (groups, local_len, HEADS, HD)
    rounded_sum, unused = lax.scan(attend_step, jnp.zeros(head_shape, f32), jnp.arange(count))
    attended = rounded_sum.reshape(rows_total, width).astype(bf16)
    pre_act = jnp.dot(normed_mlp, weight_in, preferred_element_type=f32) + bias_in.astype(f32)
    activated = jax.nn.gelu(pre_act, approximate=False).astype(bf16)
    output = (
        flat_in
        + jnp.dot(attended, weight_attn, preferred_element_type=f32)
        + jnp.dot(activated, weight_out, preferred_element_type=f32)
        + bias_out.astype(f32)
    )
    (
        gain_attn,
        shift_attn,
        weight_qkv,
        bias_qkv,
        weight_attn,
        bias_out,
        gain_mlp,
        shift_mlp,
        weight_in,
        bias_in,
        weight_out,
    ) = params
    grad_out = cotangent.reshape(rows_total, width)
    grad_bias_out = jnp.sum(grad_out.astype(f32), axis=0)
    grad_weight_out = jnp.einsum("rf,rd->fd", activated, grad_out, preferred_element_type=f32)
    grad_act = jnp.einsum("rd,fd->rf", grad_out, weight_out, preferred_element_type=f32)
    unused, gelu_back = jax.vjp(partial(jax.nn.gelu, approximate=False), pre_act)
    grad_pre = gelu_back(grad_act)[0].astype(bf16)
    grad_weight_in = jnp.einsum("rd,rf->df", normed_mlp, grad_pre, preferred_element_type=f32)
    grad_bias_in = jnp.sum(grad_pre.astype(f32), axis=0)
    grad_normed_mlp = jnp.einsum("rf,df->rd", grad_pre, weight_in, preferred_element_type=f32)
    grad_weight_attn = jnp.einsum("ra,rd->ad", attended, grad_out, preferred_element_type=f32)
    grad_att = (
        jnp.einsum("rd,ad->ra", grad_out, weight_attn, preferred_element_type=f32)
        .astype(bf16)
        .reshape(head_shape)
    )
    delta = jnp.einsum(
        "gqhd,gqhd->ghq", grad_att.astype(f32), rounded_sum, precision=lax.Precision.HIGHEST
    )

    def back_step(carry, index):
        keys_blk, values_blk, mask = key_block(index)
        rounded, grad_scores = block_grads(
            queries, grad_att, log_total, delta, mask, keys_blk, values_blk
        )
        carry = carry + jnp.einsum(
            "ghqk,gkhd->gqhd", grad_scores, keys_blk, preferred_element_type=f32
        )
        key_term = jnp.einsum("ghqk,gqhd->gkhd", grad_scores, queries, preferred_element_type=f32)
        value_term = jnp.einsum("ghqk,gqhd->gkhd", rounded, grad_att, preferred_element_type=f32)
        return (carry, (key_term, value_term))

    grad_queries, (key_terms, value_terms) = lax.scan(
        back_step, jnp.zeros(head_shape, f32), jnp.arange(count)
    )
    key_sums, value_sums = (
        lax.psum_scatter(
            key_terms.astype(jnp.bfloat16), "ctx", scatter_dimension=0, tiled=True
        ).astype(jnp.float32),
        lax.psum_scatter(
            value_terms.astype(jnp.bfloat16), "ctx", scatter_dimension=0, tiled=True
        ).astype(jnp.float32),
    )
    grad_keys = jnp.transpose(key_sums, (1, 0, 2, 3, 4)).reshape(head_shape)
    grad_values = jnp.transpose(value_sums, (1, 0, 2, 3, 4)).reshape(head_shape)
    grad_q_pre = unrotate(grad_queries * scale, cosine, sine).reshape(rows_total, width)
    grad_k_pre = unrotate(grad_keys, cosine, sine).reshape(rows_total, width)
    grad_projected = jnp.concatenate(
        [grad_q_pre, grad_k_pre, grad_values.reshape(rows_total, width)], axis=1
    ).astype(bf16)
    grad_weight_qkv = jnp.einsum(
        "rd,re->de", normed_attn, grad_projected, preferred_element_type=f32
    )
    grad_bias_qkv = jnp.sum(grad_projected.astype(f32), axis=0)
    grad_normed_attn = jnp.einsum(
        "re,de->rd", grad_projected, weight_qkv, preferred_element_type=f32
    )
    unused, norm_back_attn = jax.vjp(
        layer_norm, flat_in, gain_attn.astype(f32), shift_attn.astype(f32)
    )
    grad_in_attn, grad_gain_attn, grad_shift_attn = norm_back_attn(grad_normed_attn)
    unused, norm_back_mlp = jax.vjp(
        layer_norm, flat_in, gain_mlp.astype(f32), shift_mlp.astype(f32)
    )
    grad_in_mlp, grad_gain_mlp, grad_shift_mlp = norm_back_mlp(grad_normed_mlp)
    grad_inputs = (grad_out.astype(f32) + grad_in_attn + grad_in_mlp).reshape(
        groups, local_len, width
    )
    sums = (
        lax.psum_scatter(grad_gain_attn, ("fsdp", "ctx"), scatter_dimension=0, tiled=True),
        lax.psum_scatter(grad_shift_attn, ("fsdp", "ctx"), scatter_dimension=0, tiled=True),
        lax.psum_scatter(grad_weight_qkv, ("fsdp", "ctx"), scatter_dimension=0, tiled=True),
        lax.psum_scatter(grad_bias_qkv, ("fsdp", "ctx"), scatter_dimension=0, tiled=True),
        lax.psum_scatter(grad_weight_attn, ("fsdp", "ctx"), scatter_dimension=0, tiled=True),
        lax.psum_scatter(grad_bias_out, ("fsdp", "ctx"), scatter_dimension=0, tiled=True),
        lax.psum_scatter(grad_gain_mlp, ("fsdp", "ctx"), scatter_dimension=0, tiled=True),
        lax.psum_scatter(grad_shift_mlp, ("fsdp", "ctx"), scatter_dimension=0, tiled=True),
        lax.psum_scatter(grad_weight_in, ("fsdp", "ctx"), scatter_dimension=0, tiled=True),
        lax.psum_scatter(grad_bias_in, ("fsdp", "ctx"), scatter_dimension=0, tiled=True),
        lax.psum_scatter(grad_weight_out, ("fsdp", "ctx"), scatter_dimension=0, tiled=True),
    )
    result = output.reshape(groups, local_len, width).astype(bf16)
    return (
        result,
        grad_inputs,
        sums[0],
        sums[1],
        sums[2],
        sums[3],
        sums[4],
        sums[5],
        sums[6],
        sums[7],
        sums[8],
        sums[9],
        sums[10],
    )


def solution(mesh):
    in_specs = (
        P("fsdp", "ctx", None),
        P("fsdp", "ctx", None),
        P("fsdp", "ctx"),
        P("fsdp", "ctx"),
        P("fsdp"),
        P("fsdp"),
        P("fsdp", None),
        P("fsdp"),
        P("fsdp", None),
        P("fsdp"),
        P("fsdp"),
        P("fsdp"),
        P("fsdp", None),
        P("fsdp"),
        P("fsdp", None),
    )
    out_specs = (
        P("fsdp", "ctx", None),
        P("fsdp", "ctx", None),
        P(("fsdp", "ctx")),
        P(("fsdp", "ctx")),
        P(("fsdp", "ctx"), None),
        P(("fsdp", "ctx")),
        P(("fsdp", "ctx"), None),
        P(("fsdp", "ctx")),
        P(("fsdp", "ctx")),
        P(("fsdp", "ctx")),
        P(("fsdp", "ctx"), None),
        P(("fsdp", "ctx")),
        P(("fsdp", "ctx"), None),
    )
    return jax.shard_map(local, mesh=mesh, in_specs=in_specs, out_specs=out_specs, check_vma=False)
```

profile of v0, /device:TPU:0, one launch (start us, length us, event | category | flops | bytes accessed | tf_op | source)
XLA Modules:
  0.0 2799.0 jit_solution(5648398646766879114)
XLA Ops:
  8.0 10.3 all-gather
  40.2 18.0 all-gather.14.cloned.1.call-done
  98.3 13.3 all_gather.51
  111.5 18.1 all_gather.50
  133.6 107.9 %all-gather.18.cloned.1.call-done = bf16[1,4096,16,64]{1,3,2,0:T(8,128)(2,1)} async-done(((bf16[1,1024,16,64]{1,3,2,0:T(8,128)(2,1)}), bf16[1,4096,16,64]{1,3,2,0:T(8,128)(2,1)}) %all-gather.18.cloned.1.call-update) | async-done | bytes 8388624 | tf_op jit(solution)/shard_map/all_gather | solution.py:151
  241.4 326.4 %while.39 = (s32[]{:T(128)}, f32[1,16,1024]{2,1,0:T(8,128)S(1)}, f32[1,16,1024]{2,1,0:T(8,128)S(1)}, s32[16]{0:T(128)S(1)}, s32[1,4096]{1,0:T(1,128)S(1)}, /*ind...) while((s32[]{:T(128)}, f32[1,16,1024]{2,1,0:T(8,128)S(1)}, ...), condition=%wide.region_5.6_spmd.clone, body=%wide.region_2.5_spmd.clone.sunk | while | flops 563167488 | bytes 37830352 | solution.py:176
  243.1 11.0 fusion.159
  567.9 167.2 %while.40 = (s32[]{:T(128)}, f32[1,1024,16,64]{1,3,2,0:T(8,128)}, s32[16]{0:T(128)S(1)}, bf16[1,4096,16,64]{1,3,2,0:T(8,128)(2,1)}, s32[1,4096]{1,0:T(1,128)S(1)...) while((s32[]{:T(128)}, f32[1,1024,16,64]{1,3,2,0:T(8,128)}, ...), condition=%wide.region_7.8_spmd.clone, body=%wide.region_6.7_spmd.clone.sunk | while | flops 1089470720 | bytes 12141780 | solution.py:192
  742.4 715.6 %while.41 = (s32[]{:T(128)}, f32[1,1024,16,64]{1,3,2,0:T(8,128)}, bf16[16,1,256,16,64]{2,4,3,1,0:T(8,128)(2,1)}, bf16[16,1,256,16,64]{2,4,3,1,0:T(8,128)(2,1)}, ...) while((s32[]{:T(128)}, f32[1,1024,16,64]{1,3,2,0:T(8,128)}, ...), condition=%wide.region_9.10_spmd.clone, body=%wide.region_8.9_spmd.clone.sunk | while | flops 2721054976 | bytes 138887984 | solution.py:246
  776.0 10.0 fusion.176
  865.7 9.9 fusion.176
  910.5 9.9 fusion.176
  955.3 9.9 fusion.176
  1134.5 9.9 fusion.176
  1179.3 9.9 fusion.176
  1224.1 9.9 fusion.176
  1268.9 9.9 fusion.176
  1313.7 9.9 fusion.176
  1494.4 50.9 %multiply_convert_fusion = (bf16[1024,4096]{1,0:T(8,128)(2,1)}, f32[1024,4096]{1,0:T(8,128)}, f32[1024,4096]{1,0:T(8,128)}) fusion(f32[4096]{0:T(1024)S(1)} %bitcast.419, bf16[1024,4096]{1,0:T(8,128)(2,1)} %all-gather.22.cloned.1.call-done, bf16[1,1024,1024]{2,1,0:T(8,128)(2,1)S(1)} %copy-done.3, f32[1024]{0:T(1024)S(1)} %bitcast.424, ...), kind=kOutput, calls=%fused_computation.67 | convolution fusion | flops 8873050112 | bytes 52461568 | tf_op jit(solution)/shard_map/dot_general | solution.py:194
  1545.3 24.3 convert_reduce_fusion
  1569.6 15.1 fusion.109
  1584.7 16.6 fusion.95
  1613.3 136.2 %reduce-scatter.9.cloned.1.call-done = bf16[4,1,256,16,64]{2,4,3,1,0:T(8,128)(2,1)} async-done(((bf16[16,1,256,16,64]{2,4,3,1,0:T(8,128)(2,1)}), bf16[4,1,256,16,64]{2,4,3,1,0:T(8,128)(2,1)}) %reduce-scatter.9.cloned.1.call-update) | async-done | bytes 2097168 | tf_op jit(solution)/shard_map/reduce_scatter | solution.py:253
  1759.0 11.7 fusion.113
  1780.0 13.1 fusion.124
  1795.5 14.9 fusion.94
  1810.4 13.5 fusion.120
  1838.5 41.4 %all-reduce.7 = (f32[1024]{0:T(1024)S(1)}, f32[1024]{0:T(1024)S(1)}, f32[3072]{0:T(1024)S(1)}, f32[1024]{0:T(1024)S(1)}, f32[1024]{0:T(1024)S(1)}, /*index=5*/f32[1024]{0:T(1024)S(1)}, f32[4096]{0:T(1024)S(1)}) all-reduce(f32[1024]{0:T(1024)S(1)} %get-tuple-element.356, ...), channel_id=4, replica_groups=mesh['fsdp'=8,'ctx'=4] {'fsdp','ctx'}, use_global_device_ids=true, to_apply=%region_17.18.clone | all-reduce | flops 12288 | bytes 98304
  1884.0 17.0 reduce-scatter.13.cloned.1.call-done
  1901.0 366.0 %reduce-scatter.15.cloned.1.call-done = f32[32,4096]{1,0:T(8,128)} async-done(((f32[1024,4096]{1,0:T(8,128)}), f32[32,4096]{1,0:T(8,128)}) %reduce-scatter.15.cloned.1.call-update) | async-done | bytes 524304 | tf_op jit(solution)/shard_map/reduce_scatter | solution.py:291
  2267.0 365.1 %reduce-scatter.17.cloned.1.call-done = f32[128,1024]{1,0:T(8,128)} async-done(((f32[4096,1024]{1,0:T(8,128)}), f32[128,1024]{1,0:T(8,128)}) %reduce-scatter.17.cloned.1.call-update) | async-done | bytes 524304 | tf_op jit(solution)/shard_map/reduce_scatter | solution.py:293
  2632.0 159.8 %reduce-scatter.11.cloned.1.call-done = f32[32,3072]{1,0:T(8,128)} async-done(((f32[1024,3072]{1,0:T(8,128)}), f32[32,3072]{1,0:T(8,128)}) %reduce-scatter.11.cloned.1.call-update) | async-done | bytes 393232 | tf_op jit(solution)/shard_map/reduce_scatter | solution.py:285
  (596 shorter events, 1236.7 us)
Async XLA Ops:
  7.2 31.5 %copy-start.2 = (bf16[1,1024,1024]{2,1,0:T(8,128)(2,1)S(1)}, bf16[1,1024,1024]{2,1,0:T(8,128)(2,1)}, u32[]{:S(2)}) copy-start(bf16[1,1024,1024]{2,1,0:T(8,128)(2,1)} %param.21) | copy-start | bytes 6291460
  7.2 51.0 %all-gather.14.cloned.1.call-start = ((), (), s32[]{:S(2)}) async-start(), calls=%async_computation.6 | async-start | bytes 7077888 | tf_op jit(solution)/shard_map/all_gather | solution.py:104
  7.9 233.5 %all-gather.18.cloned.1.call-start = ((), (), s32[]{:S(2)}) async-start(), calls=%async_computation.8 | async-start | bytes 10485760 | tf_op jit(solution)/shard_map/all_gather | solution.py:151
  18.3 48.9 %copy-start.27 = (f32[8,1,128]{2,1,0:T(1,128)}, f32[8,1,128]{2,1,0:T(1,128)S(1)}, u32[]{:S(2)}) copy-start(f32[8,1,128]{2,1,0:T(1,128)S(1)} %convert_element_type.150) | copy-start | bytes 12292
  26.9 40.3 %copy-start.33 = (f32[8,1,128]{2,1,0:T(1,128)}, f32[8,1,128]{2,1,0:T(1,128)S(1)}, u32[]{:S(2)}) copy-start(f32[8,1,128]{2,1,0:T(1,128)S(1)} %convert_element_type.151) | copy-start | bytes 12292
  38.7 28.5 %copy-start.25 = (f32[1024]{0:T(1024)}, f32[1024]{0:T(1024)S(1)}, u32[]{:S(2)}) copy-start(f32[1024]{0:T(1024)S(1)} %broadcast_multiply_fusion.1) | copy-start | bytes 12292
  40.0 27.3 copy-start.29
  40.2 46.9 %copy-start.21 = (f32[1024,8]{0,1:T(8,128)}, f32[1024,8]{0,1:T(8,128)S(1)}, u32[]{:S(2)}) copy-start(f32[1024,8]{0,1:T(8,128)S(1)} %get-tuple-element.464) | copy-start | bytes 98308
  40.2 46.9 %copy-start.23 = (f32[1024,8]{0,1:T(8,128)}, f32[1024,8]{0,1:T(8,128)S(1)}, u32[]{:S(2)}) copy-start(f32[1024,8]{0,1:T(8,128)S(1)} %get-tuple-element.465) | copy-start | bytes 98308
  91.3 476.6 %all-gather.16.cloned.1.call-start = ((), (), s32[]{:S(2)}) async-start(), calls=%async_computation.7 | async-start | bytes 10485760 | tf_op jit(solution)/shard_map/all_gather | solution.py:152
  93.9 17.7 copy-start.20
  96.5 638.7 %all-gather.20.cloned.1.call-start = ((), (), s32[]{:S(2)}) async-start(), calls=%async_computation.9 | async-start | bytes 2359296 | tf_op jit(solution)/shard_map/all_gather | solution.py:106
  97.0 1395.9 %all-gather.22.cloned.1.call-start = ((), (), s32[]{:S(2)}) async-start(), calls=%async_computation.10 | async-start | bytes 9437184 | tf_op jit(solution)/shard_map/all_gather | solution.py:110
  97.6 1447.7 %all-gather.24.cloned.1.call-start = ((), (), s32[]{:S(2)}) async-start(), calls=%async_computation.11 | async-start | bytes 9437184 | tf_op jit(solution)/shard_map/all_gather | solution.py:112
  98.2 1509.3 %reduce-scatter.7.cloned.1.call-start = ((), (), s32[]{:S(2)}) async-start(), calls=%async_computation.12 | async-start | bytes 10485760 | tf_op jit(solution)/shard_map/reduce_scatter | solution.py:250
  832.4 9.3 copy-start.1
  877.2 9.3 copy-start.1
  922.1 9.3 copy-start.1
  1458.0 291.5 %reduce-scatter.9.cloned.1.call-start = ((), (), s32[]{:S(2)}) async-start(), calls=%async_computation.13 | async-start | bytes 10485760 | tf_op jit(solution)/shard_map/reduce_scatter | solution.py:253
  1458.0 9.6 copy-start.35
  1458.0 18.4 copy-start.37
  1458.7 29.7 %copy-start.15 = (bf16[1,1024,1024]{2,1,0:T(8,128)(2,1)S(1)}, bf16[1,1024,1024]{2,1,0:T(8,128)(2,1)}, u32[]{:S(2)}) copy-start(bf16[1,1024,1024]{2,1,0:T(8,128)(2,1)} %param.22) | copy-start | bytes 6291460
  1458.7 442.3 %reduce-scatter.13.cloned.1.call-start = ((), (), s32[]{:S(2)}) async-start(), calls=%async_computation.15 | async-start | bytes 4325376 | tf_op jit(solution)/shard_map/reduce_scatter | solution.py:287
  1492.8 774.1 %reduce-scatter.15.cloned.1.call-start = ((), (), s32[]{:S(2)}) async-start(), calls=%async_computation.16 | async-start | bytes 17301504 | tf_op jit(solution)/shard_map/reduce_scatter | solution.py:291
  1584.6 1047.4 %reduce-scatter.17.cloned.1.call-start = ((), (), s32[]{:S(2)}) async-start(), calls=%async_computation.17 | async-start | bytes 17301504 | tf_op jit(solution)/shard_map/reduce_scatter | solution.py:293
  1601.3 1190.5 %reduce-scatter.11.cloned.1.call-start = ((), (), s32[]{:S(2)}) async-start(), calls=%async_computation.14 | async-start | bytes 12976128 | tf_op jit(solution)/shard_map/reduce_scatter | solution.py:285
  1613.3 140.1 %copy-start.22 = (f32[1024,8]{0,1:T(8,128)S(1)}, f32[1024,8]{0,1:T(8,128)}, u32[]{:S(2)}) copy-start(f32[1024,8]{0,1:T(8,128)} %copy-done.21) | copy-start | bytes 98308
  1613.3 140.1 %copy-start.24 = (f32[1024,8]{0,1:T(8,128)S(1)}, f32[1024,8]{0,1:T(8,128)}, u32[]{:S(2)}) copy-start(f32[1024,8]{0,1:T(8,128)} %copy-done.23) | copy-start | bytes 98308
  1780.0 13.1 copy-start.18
  1780.0 13.1 copy-start.39
  1795.5 14.9 copy-start.8
  1810.4 13.5 copy-start.32
  (50 other events, 233.5 us)
Sparse Core Ops, SparseCore 0:
  9.9 48.2 all-gather.13
  91.4 149.9 all-gather.17
  243.6 147.9 all-gather.15
  393.3 26.0 all-gather.19
  421.1 54.3 all-gather.21
  477.3 54.3 all-gather.23
  1458.1 143.7 reduce-scatter.6
  1604.2 145.1 reduce-scatter.8
  1752.3 148.6 reduce-scatter.12
  1903.7 363.2 reduce-scatter.14
  2269.8 362.1 reduce-scatter.16
  2638.5 153.3 reduce-scatter.10
where the time goes:
time: 2810 us; the launch traced here: 2800 us
  waiting for transfers between devices  1170 us (42%)
  matrix products  1110 us (40%)
  other arithmetic  202 us (7%)
  blocking collectives  134 us (5%)
  local copies, waits for them, and re-layouts  129 us (5%)
  loops' own time  34 us (1%)
    reduce_scatter x1, waiting for transfers between devices, local(): lax.psum_scatter(grad_weight_in, ('fsdp', 'ctx'), scatter_dimension=0, ti...  366 us
    reduce_scatter x1, waiting for transfers between devices, local(): lax.psum_scatter(grad_weight_out, ('fsdp', 'ctx'), scatter_dimension=0, t...  365 us
    dot_general x32, matrix products, scores_of(): jnp.einsum('gqhd,gkhd->ghqk', queries, keys_blk, preferred_element_type=j...  299 us
    reduce_scatter x1, waiting for transfers between devices, local(): lax.psum_scatter(grad_weight_qkv, ('fsdp', 'ctx'), scatter_dimension=0, t...  160 us
    dot_general x16, matrix products, back_step(): jnp.einsum('ghqk,gqhd->gkhd', rounded, grad_att, preferred_element_type=f32)  158 us
    reduce_sum x16, other arithmetic, total_step(): jnp.sum(jnp.where(mask, jnp.exp(scores - fresh[..., None]), 0.0), axis=-1)  149 us
    dot_general x16, matrix products, block_grads(): jnp.einsum('gqhd,gkhd->ghqk', grad_att, values_blk, preferred_element_typ...  144 us
    dot_general x16, matrix products, attend_step(): jnp.einsum('ghqk,gkhd->gqhd', probs.astype(bf16), values_blk, preferred_e...  141 us
  transfers between devices with their start and end apart: 12, of which 7 were waited for; matrix products, arithmetic and copies ran while one was open for 48% of the time, Pallas kernels for 0%

commit v1 on v0

--- a/solution.py
+++ b/solution.py
@@ -85,6 +85,37 @@
     b_in,
     w_out,
 ):
+
+    def recast_loads_on_mesh(along_dim, block_in):
+        ax_name = "ctx"
+        g_now = jax.lax.axis_size(ax_name)
+        then = jax.lax.axis_index(ax_name)
+        local_now, block_next, formed = (g_now, then, block_in.shape[along_dim])
+        all_blocks = [
+            dd * local_now if idx == along_dim else dd for idx, dd in enumerate(block_in.shape)
+        ]
+        b_now = lax.dynamic_update_slice_in_dim(
+            jnp.zeros(all_blocks, block_in.dtype), block_in, block_next * formed, axis=along_dim
+        )
+        w2 = block_out = block_in
+        for rr in range(1, local_now // 2 + 1):
+            high = range(local_now)
+            reply = map(lambda idx: (idx, (idx + 1) % local_now), high)
+            w2 = jax.lax.ppermute(w2, axis_name=ax_name, perm=list(reply))
+            b_now = lax.dynamic_update_slice_in_dim(
+                b_now, w2, (block_next - rr) % local_now * formed, axis=along_dim
+            )
+            if 2 * rr < local_now:
+                block_out = jax.lax.ppermute(
+                    block_out,
+                    axis_name=ax_name,
+                    perm=list(map(lambda idx: (idx, (idx - 1) % local_now), range(local_now))),
+                )
+                b_now = lax.dynamic_update_slice_in_dim(
+                    b_now, block_out, (block_next + rr) % local_now * formed, axis=along_dim
+                )
+        return b_now
+
     shards = (
         ln1_gain,
         ln1_bias,
@@ -148,7 +179,7 @@
     keys_own = rotate(split_heads(projected[:, width : 2 * width]), cosine, sine).astype(bf16)
     values_own = split_heads(projected[:, 2 * width :]).astype(bf16)
     keys_all, values_all = (
-        lax.all_gather(keys_own, "ctx", axis=1, tiled=True),
+        recast_loads_on_mesh(1, keys_own),
         lax.all_gather(values_own, "ctx", axis=1, tiled=True),
     )
 

time: 2810 us -> 2960 us (1.053)
  starting transfers between devices: 0.48 us -> 86.5 us
  blocking collectives: 134 us -> 196 us
    all_gather x1 -> x0, waiting for transfers between devices: 108 us -> none  [local(): lax.all_gather(keys_own, 'ctx', axis=1, tiled=True)]
    ppermute x0 -> x3, waiting for transfers between devices: none -> 91.7 us  [the longest x2 91.7 us: recast_loads_on_mesh(): w2 = jax.lax.ppermute(w2, axis_name=ax_name, perm=list(reply))]
    ppermute x0 -> x3, starting transfers between devices: none -> 86.1 us  [the longest x2 83.7 us: recast_loads_on_mesh(): w2 = jax.lax.ppermute(w2, axis_name=ax_name, perm=list(reply))]
    all_gather x1, blocking collectives: 13.3 us -> 79.9 us  [local(): lax.all_gather(positions, 'ctx', axis=1, tiled=True)]
  transfers between devices with their start and end apart: 12 -> 14, of which waited for: 7 -> 7; matrix products, arithmetic and copies ran while one was open for 48% -> 47% of each run, Pallas kernels for 0% -> 0%
where the time goes in v1:
time: 2960 us; the launch traced here: 2950 us
  waiting for transfers between devices  1160 us (39%)
  matrix products  1110 us (38%)
  other arithmetic  203 us (7%)
  blocking collectives  196 us (7%)
  local copies, waits for them, and re-layouts  147 us (5%)
  starting transfers between devices  86.5 us (3%)
  loops' own time  34.3 us (1%)
    reduce_scatter x1, waiting for transfers between devices, local(): lax.psum_scatter(grad_weight_in, ('fsdp', 'ctx'), scatter_dimension=0, ti...  366 us
    reduce_scatter x1, waiting for transfers between devices, local(): lax.psum_scatter(grad_weight_out, ('fsdp', 'ctx'), scatter_dimension=0, t...  365 us
    dot_general x32, matrix products, scores_of(): jnp.einsum('gqhd,gkhd->ghqk', queries, keys_blk, preferred_element_type=j...  297 us
    reduce_scatter x1, waiting for transfers between devices, local(): lax.psum_scatter(grad_weight_qkv, ('fsdp', 'ctx'), scatter_dimension=0, t...  160 us
    dot_general x16, matrix products, back_step(): jnp.einsum('ghqk,gqhd->gkhd', rounded, grad_att, preferred_element_type=f32)  159 us
    reduce_sum x16, other arithmetic, total_step(): jnp.sum(jnp.where(mask, jnp.exp(scores - fresh[..., None]), 0.0), axis=-1)  150 us
    dot_general x16, matrix products, block_grads(): jnp.einsum('gqhd,gkhd->ghqk', grad_att, values_blk, preferred_element_typ...  144 us
    dot_general x16, matrix products, attend_step(): jnp.einsum('ghqk,gkhd->gqhd', probs.astype(bf16), values_blk, preferred_e...  141 us
  transfers between devices with their start and end apart: 14, of which 7 were waited for; matrix products, arithmetic and copies ran while one was open for 47% of the time, Pallas kernels for 0%

profile of v1, /device:TPU:0, one launch (start us, length us, event | category | flops | bytes accessed | tf_op | source)
XLA Modules:
  0.0 2949.2 jit_solution(5807888344387737021)
XLA Ops:
  8.0 10.3 all-gather
  38.9 19.3 all-gather.13.cloned.1.call-done
  111.9 91.7 %collective-permute-done = bf16[1,1024,16,64]{1,3,2,0:T(8,128)(2,1)} collective-permute-done((bf16[1,1024,16,64]{1,3,2,0:T(8,128)(2,1)}, bf16[1,1024,16,64]{1,3,2,0:T(8,128)(2,1)}, u32[]{:S(2)}, u32[]{:S(2)}) %collective-permute-start) | collective-permute-done | bytes 2097184 | tf_op jit(solution)/shard_map/ppermute | solution.py:104
  203.5 82.3 %collective-permute-start.2 = (bf16[1,1024,16,64]{1,3,2,0:T(8,128)(2,1)}, bf16[1,1024,16,64]{1,3,2,0:T(8,128)(2,1)}, u32[]{:S(2)}, u32[]{:S(2)}) collective-permute-start(bf16[1,1024,16,64]{1,3,2,0:T(8,128)(2,1)} %collective-permute-done), channel_id=1, source_target_pairs={{0,1},{1,2},{2,3},{3,0},{4,5},{5,6},{6,7},{7,4},{8,9},{9,10},{10,1... | collective-permute-start | bytes 6291464 | tf_op jit(solution)/shard_map/ppermute | solution.py:104
  286.0 79.9 %all_gather.48 = s32[1,4096]{1,0:T(1,128)S(1)} all-gather(s32[1,1024]{1,0:T(1,128)S(1)} %copy-done.19), channel_id=1, replica_groups=mesh['fsdp'=8,'ctx'=4] {'ctx'}, dimensions={1}, use_global_device_ids=true | all-gather | bytes 20480 | tf_op jit(solution)/shard_map/all_gather | solution.py:149
  365.9 13.1 all_gather.47
  392.7 326.5 %while.39 = (s32[]{:T(128)}, f32[1,16,1024]{2,1,0:T(8,128)S(1)}, f32[1,16,1024]{2,1,0:T(8,128)S(1)}, s32[16]{0:T(128)S(1)}, s32[1,4096]{1,0:T(1,128)S(1)}, /*ind...) while((s32[]{:T(128)}, f32[1,16,1024]{2,1,0:T(8,128)S(1)}, ...), condition=%wide.region_5.6_spmd.clone, body=%wide.region_2.5_spmd.clone.sunk | while | flops 563167488 | bytes 37830352 | solution.py:207
  424.3 10.3 select_reduce_fusion.2
  445.6 10.6 select_reduce_fusion.2
  719.3 167.3 %while.40 = (s32[]{:T(128)}, f32[1,1024,16,64]{1,3,2,0:T(8,128)}, s32[16]{0:T(128)S(1)}, bf16[1,4096,16,64]{1,3,2,0:T(8,128)(2,1)}, s32[1,4096]{1,0:T(1,128)S(1)...) while((s32[]{:T(128)}, f32[1,1024,16,64]{1,3,2,0:T(8,128)}, ...), condition=%wide.region_7.8_spmd.clone, body=%wide.region_6.7_spmd.clone.sunk | while | flops 1089470720 | bytes 12141780 | solution.py:223
  893.8 715.8 %while.41 = (s32[]{:T(128)}, f32[1,1024,16,64]{1,3,2,0:T(8,128)}, bf16[16,1,256,16,64]{2,4,3,1,0:T(8,128)(2,1)}, bf16[16,1,256,16,64]{2,4,3,1,0:T(8,128)(2,1)}, ...) while((s32[]{:T(128)}, f32[1,1024,16,64]{1,3,2,0:T(8,128)}, ...), condition=%wide.region_9.10_spmd.clone, body=%wide.region_8.9_spmd.clone.sunk | while | flops 2721054976 | bytes 138887984 | solution.py:277
  927.5 10.0 fusion.176
  1062.0 9.9 fusion.176
  1286.0 9.9 fusion.176
  1375.5 9.9 fusion.176
  1420.4 9.9 fusion.176
  1465.2 9.9 fusion.176
  1510.0 9.9 fusion.176
  1646.1 51.1 %multiply_convert_fusion = (bf16[1024,4096]{1,0:T(8,128)(2,1)}, f32[1024,4096]{1,0:T(8,128)}, f32[1024,4096]{1,0:T(8,128)}) fusion(f32[4096]{0:T(1024)S(1)} %bitcast.419, bf16[1024,4096]{1,0:T(8,128)(2,1)} %all-gather.19.cloned.1.call-done, bf16[1,1024,1024]{2,1,0:T(8,128)(2,1)S(1)} %copy-done.3, f32[1024]{0:T(1024)S(1)} %bitcast.424, ...), kind=kOutput, calls=%fused_computation.67 | convolution fusion | flops 8873050112 | bytes 52461568 | tf_op jit(solution)/shard_map/dot_general | solution.py:225
  1697.2 24.2 convert_reduce_fusion
  1721.4 15.2 fusion.109
  1736.7 16.6 fusion.95
  1765.0 135.0 %reduce-scatter.9.cloned.1.call-done = bf16[4,1,256,16,64]{2,4,3,1,0:T(8,128)(2,1)} async-done(((bf16[16,1,256,16,64]{2,4,3,1,0:T(8,128)(2,1)}), bf16[4,1,256,16,64]{2,4,3,1,0:T(8,128)(2,1)}) %reduce-scatter.9.cloned.1.call-update) | async-done | bytes 2097168 | tf_op jit(solution)/shard_map/reduce_scatter | solution.py:284
  1909.5 11.7 fusion.113
  1930.6 13.1 fusion.124
  1946.1 14.9 fusion.94
  1961.0 13.5 fusion.120
  1989.1 41.5 %all-reduce.7 = (f32[1024]{0:T(1024)S(1)}, f32[1024]{0:T(1024)S(1)}, f32[3072]{0:T(1024)S(1)}, f32[1024]{0:T(1024)S(1)}, f32[1024]{0:T(1024)S(1)}, /*index=5*/f32[1024]{0:T(1024)S(1)}, f32[4096]{0:T(1024)S(1)}) all-reduce(f32[1024]{0:T(1024)S(1)} %get-tuple-element.356, ...), channel_id=4, replica_groups=mesh['fsdp'=8,'ctx'=4] {'fsdp','ctx'}, use_global_device_ids=true, to_apply=%region_17.18.clone | all-reduce | flops 12288 | bytes 98304
  2034.7 17.0 reduce-scatter.13.cloned.1.call-done
  2051.7 365.7 %reduce-scatter.15.cloned.1.call-done = f32[32,4096]{1,0:T(8,128)} async-done(((f32[1024,4096]{1,0:T(8,128)}), f32[32,4096]{1,0:T(8,128)}) %reduce-scatter.15.cloned.1.call-update) | async-done | bytes 524304 | tf_op jit(solution)/shard_map/reduce_scatter | solution.py:322
  2417.4 364.9 %reduce-scatter.17.cloned.1.call-done = f32[128,1024]{1,0:T(8,128)} async-done(((f32[4096,1024]{1,0:T(8,128)}), f32[128,1024]{1,0:T(8,128)}) %reduce-scatter.17.cloned.1.call-update) | async-done | bytes 524304 | tf_op jit(solution)/shard_map/reduce_scatter | solution.py:324
  2782.3 160.0 %reduce-scatter.11.cloned.1.call-done = f32[32,3072]{1,0:T(8,128)} async-done(((f32[1024,3072]{1,0:T(8,128)}), f32[32,3072]{1,0:T(8,128)}) %reduce-scatter.11.cloned.1.call-update) | async-done | bytes 393232 | tf_op jit(solution)/shard_map/reduce_scatter | solution.py:316
  (603 shorter events, 1268.6 us)
Async XLA Ops:
  7.2 30.4 %copy-start.2 = (bf16[1,1024,1024]{2,1,0:T(8,128)(2,1)S(1)}, bf16[1,1024,1024]{2,1,0:T(8,128)(2,1)}, u32[]{:S(2)}) copy-start(bf16[1,1024,1024]{2,1,0:T(8,128)(2,1)} %param.21) | copy-start | bytes 6291460
  7.2 51.0 %all-gather.13.cloned.1.call-start = ((), (), s32[]{:S(2)}) async-start(), calls=%async_computation.6 | async-start | bytes 7077888 | tf_op jit(solution)/shard_map/all_gather | solution.py:135
  7.9 711.3 %all-gather.15.cloned.1.call-start = ((), (), s32[]{:S(2)}) async-start(), calls=%async_computation.7 | async-start | bytes 10485760 | tf_op jit(solution)/shard_map/all_gather | solution.py:183
  18.3 48.9 %copy-start.27 = (f32[8,1,128]{2,1,0:T(1,128)}, f32[8,1,128]{2,1,0:T(1,128)S(1)}, u32[]{:S(2)}) copy-start(f32[8,1,128]{2,1,0:T(1,128)S(1)} %convert_element_type.150) | copy-start | bytes 12292
  26.9 40.3 %copy-start.33 = (f32[8,1,128]{2,1,0:T(1,128)}, f32[8,1,128]{2,1,0:T(1,128)S(1)}, u32[]{:S(2)}) copy-start(f32[8,1,128]{2,1,0:T(1,128)S(1)} %convert_element_type.151) | copy-start | bytes 12292
  37.6 29.6 %copy-start.25 = (f32[1024]{0:T(1024)}, f32[1024]{0:T(1024)S(1)}, u32[]{:S(2)}) copy-start(f32[1024]{0:T(1024)S(1)} %broadcast_multiply_fusion.1) | copy-start | bytes 12292
  38.9 28.3 copy-start.29
  74.7 811.9 %all-gather.17.cloned.1.call-start = ((), (), s32[]{:S(2)}) async-start(), calls=%async_computation.8 | async-start | bytes 2359296 | tf_op jit(solution)/shard_map/all_gather | solution.py:137
  75.4 1569.2 %all-gather.19.cloned.1.call-start = ((), (), s32[]{:S(2)}) async-start(), calls=%async_computation.9 | async-start | bytes 9437184 | tf_op jit(solution)/shard_map/all_gather | solution.py:141
  76.0 1621.2 %all-gather.21.cloned.1.call-start = ((), (), s32[]{:S(2)}) async-start(), calls=%async_computation.10 | async-start | bytes 9437184 | tf_op jit(solution)/shard_map/all_gather | solution.py:143
  76.3 22.0 copy-start.21
  76.3 22.0 copy-start.23
  105.2 260.7 %copy-start.20 = (s32[1,1024]{1,0:T(1,128)S(1)}, s32[1,1024]{1,0:T(1,128)}, u32[]{:S(2)}) copy-start(s32[1,1024]{1,0:T(1,128)} %param.24) | copy-start | bytes 12292
  108.0 95.5 %collective-permute-start = (bf16[1,1024,16,64]{1,3,2,0:T(8,128)(2,1)}, bf16[1,1024,16,64]{1,3,2,0:T(8,128)(2,1)}, u32[]{:S(2)}, u32[]{:S(2)}) collective-permute-start(bf16[1,1024,16,64]{1,3,2,0:T(8,128)(2,1)} %get-tuple-element.460), channel_id=1, source_target_pairs={{0,1},{1,2},{2,3},{3,0},{4,5},{5,6},{6,7},{7,4},{8,9},{9,10},{10,1... | collective-permute-start | bytes 6291464 | tf_op jit(solution)/shard_map/ppermute | solution.py:104
  109.4 276.9 %collective-permute-start.1 = (bf16[1,1024,16,64]{1,3,2,0:T(8,128)(2,1)}, bf16[1,1024,16,64]{1,3,2,0:T(8,128)(2,1)}, u32[]{:S(2)}, u32[]{:S(2)}) collective-permute-start(bf16[1,1024,16,64]{1,3,2,0:T(8,128)(2,1)} %get-tuple-element.460), channel_id=1, source_target_pairs={{0,3},{1,0},{2,1},{3,2},{4,7},{5,4},{6,5},{7,6},{8,11},{9,8},{10,9... | collective-permute-start | bytes 6291464 | tf_op jit(solution)/shard_map/ppermute | solution.py:109
  203.5 186.0 %collective-permute-start.2 = (bf16[1,1024,16,64]{1,3,2,0:T(8,128)(2,1)}, bf16[1,1024,16,64]{1,3,2,0:T(8,128)(2,1)}, u32[]{:S(2)}, u32[]{:S(2)}) collective-permute-start(bf16[1,1024,16,64]{1,3,2,0:T(8,128)(2,1)} %collective-permute-done), channel_id=1, source_target_pairs={{0,1},{1,2},{2,3},{3,0},{4,5},{5,6},{6,7},{7,4},{8,9},{9,10},{10,1... | collective-permute-start | bytes 6291464 | tf_op jit(solution)/shard_map/ppermute | solution.py:104
  285.8 1473.5 %reduce-scatter.7.cloned.1.call-start = ((), (), s32[]{:S(2)}) async-start(), calls=%async_computation.11 | async-start | bytes 10485760 | tf_op jit(solution)/shard_map/reduce_scatter | solution.py:281
  1566.3 9.3 copy-start.1
  1609.6 290.5 %reduce-scatter.9.cloned.1.call-start = ((), (), s32[]{:S(2)}) async-start(), calls=%async_computation.12 | async-start | bytes 10485760 | tf_op jit(solution)/shard_map/reduce_scatter | solution.py:284
  1609.6 9.8 copy-start.35
  1609.6 18.6 copy-start.37
  1610.3 29.8 %copy-start.15 = (bf16[1,1024,1024]{2,1,0:T(8,128)(2,1)S(1)}, bf16[1,1024,1024]{2,1,0:T(8,128)(2,1)}, u32[]{:S(2)}) copy-start(bf16[1,1024,1024]{2,1,0:T(8,128)(2,1)} %param.22) | copy-start | bytes 6291460
  1610.3 441.4 %reduce-scatter.13.cloned.1.call-start = ((), (), s32[]{:S(2)}) async-start(), calls=%async_computation.14 | async-start | bytes 4325376 | tf_op jit(solution)/shard_map/reduce_scatter | solution.py:318
  1644.6 772.8 %reduce-scatter.15.cloned.1.call-start = ((), (), s32[]{:S(2)}) async-start(), calls=%async_computation.15 | async-start | bytes 17301504 | tf_op jit(solution)/shard_map/reduce_scatter | solution.py:322
  1736.6 1045.7 %reduce-scatter.17.cloned.1.call-start = ((), (), s32[]{:S(2)}) async-start(), calls=%async_computation.16 | async-start | bytes 17301504 | tf_op jit(solution)/shard_map/reduce_scatter | solution.py:324
  1753.3 1189.0 %reduce-scatter.11.cloned.1.call-start = ((), (), s32[]{:S(2)}) async-start(), calls=%async_computation.13 | async-start | bytes 12976128 | tf_op jit(solution)/shard_map/reduce_scatter | solution.py:316
  1765.0 138.9 %copy-start.22 = (f32[1024,8]{0,1:T(8,128)S(1)}, f32[1024,8]{0,1:T(8,128)}, u32[]{:S(2)}) copy-start(f32[1024,8]{0,1:T(8,128)} %copy-done.21) | copy-start | bytes 98308
  1765.0 138.9 %copy-start.24 = (f32[1024,8]{0,1:T(8,128)S(1)}, f32[1024,8]{0,1:T(8,128)}, u32[]{:S(2)}) copy-start(f32[1024,8]{0,1:T(8,128)} %copy-done.23) | copy-start | bytes 98308
  1930.6 13.1 copy-start.18
  1930.6 13.1 copy-start.39
  1946.1 14.9 copy-start.8
  1961.0 13.5 copy-start.32
  (52 other events, 249.2 us)
Sparse Core Ops, SparseCore 0:
  9.9 48.2 all-gather.12
  74.8 257.7 all-gather.14
  334.5 26.9 all-gather.16
  363.2 54.3 all-gather.18
  419.4 54.3 all-gather.20
  1609.7 142.7 reduce-scatter.6
  1754.8 145.1 reduce-scatter.8
  1902.9 148.7 reduce-scatter.12
  2054.6 362.7 reduce-scatter.14
  2420.1 362.1 reduce-scatter.16
  2788.9 153.3 reduce-scatter.10
